TPU v7x, 32 devices: a whole 2x2x4 slice. The times are simulated.
32 devices in a mesh: dp: 8 (over y, x, core), branch: 4 (over z).
Axes of the slice: x: 2, y: 2, z: 4, core: 2. Of those that a mesh axis runs over, the one named last changes fastest.
Arguments:
- tokens: bfloat16 [8192, 2048], P(('dp', 'branch')), may hold values from -6 to 6
- doc_ids: int32 [8192], P('dp'), may hold values from 0 to 15, as said below
- real_rows: int32 [8192], P('dp'), may hold values from 0 to 1, as said below
- cotangent: bfloat16 [8192, 2048], P(('dp', 'branch')), may hold values from -6 to 6
- norm_gain: float32 [2048], P(('dp', 'branch')), may hold values from 0.5 to 1.5
- norm_shift: float32 [2048], P(('dp', 'branch')), may hold values from -2 to 2
- out_bias: float32 [2048], P(('dp', 'branch')), may hold values from -2 to 2
- w_qkv: float32 [3, 2048, 2048], P(None, 'dp', 'branch'), may hold values from -0.125 to 0.125
- b_qkv: float32 [3, 32, 64], P(None, 'branch', 'dp'), may hold values from -3 to 3
- w_out: float32 [2048, 2048], P('branch', 'dp'), may hold values from -0.75 to 0.75
- w_up: float32 [2048, 8192], P('dp', 'branch'), may hold values from -0.125 to 0.125
- b_up: float32 [64, 128], P('branch', 'dp'), may hold values from -3 to 3
- w_down: float32 [8192, 2048], P('branch', 'dp'), may hold values from -0.0625 to 0.0625
Outputs:
- block_out: bfloat16 [8192, 2048], P(('dp', 'branch'))
- tokens_grad: bfloat16 [8192, 2048], P(('dp', 'branch'))
- norm_gain_grad: float32 [2048], P(('dp', 'branch'))
- norm_shift_grad: float32 [2048], P(('dp', 'branch'))
- out_bias_grad: float32 [2048], P(('dp', 'branch'))
- w_qkv_grad: float32 [3, 2048, 2048], P(None, 'dp', 'branch')
- b_qkv_grad: float32 [3, 32, 64], P(None, 'branch', 'dp')
- w_out_grad: float32 [2048, 2048], P('branch', 'dp')
- w_up_grad: float32 [2048, 8192], P('dp', 'branch')
- b_up_grad: float32 [64, 128], P('branch', 'dp')
- w_down_grad: float32 [8192, 2048], P('branch', 'dp')
Inputs may be any that keep to these rules, and one draw needn't show every extreme that they name: `doc_ids`: within each aligned block of 1024 slots the ids start at 0 and never fall; a sequence has 64 times a power of two slots, up to 1024; some sequence has exactly 1024; all padding slots of a block share the id 1024 // 64 - 1, which real slots of a block with padding never take; the last block ends in padding. `real_rows`: within each block, the slots of whole sequences come first and are 1; the rest of the block is 0; every block holds a sequence; the last block ends in padding.
All inputs are finite; a program needn't handle non-finite values.
Results may differ from a plain program's by a relative error of at most 0.014.
Values may be sent and summed in bfloat16 or wider, within the bound.
A program may use at most 192 MiB of HBM per device.

v0:
```python
import math
import jax
import jax.numpy as jnp
from jax import lax
from jax.sharding import PartitionSpec as P

HEAD_DIM = 64
ROT = 32
NORM_EPS = 1e-05
NEGATIVE = -1e30


def positions(doc_rows):
    row_count = doc_rows.shape[0]
    row_index = jnp.arange(row_count, dtype=jnp.int32)
    change = jnp.concatenate([jnp.ones((1,), dtype=bool), doc_rows[1:] != doc_rows[:-1]])
    begins = lax.cummax(jnp.where(change, row_index, jnp.zeros_like(row_index)), axis=0)
    return row_index - begins


def rotary_tables(doc_rows):
    places = positions(doc_rows).astype(jnp.float32)
    half_rot = ROT // 2
    frequency = 10000.0 ** (-2.0 * jnp.arange(half_rot, dtype=jnp.float32) / ROT)
    angles = places[:, None] * frequency[None, :]
    return (jnp.cos(angles), jnp.sin(angles))


def rotate(values, cosine, sine_tab):
    half_rot = ROT // 2
    first_half = values[..., :half_rot]
    second_half = values[..., half_rot : 2 * half_rot]
    remain = values[..., 2 * half_rot :]
    return jnp.concatenate(
        [
            first_half * cosine - second_half * sine_tab,
            second_half * cosine + first_half * sine_tab,
            remain,
        ],
        axis=-1,
    )


def unrotate(values, cosine, sine_tab):
    half_rot = ROT // 2
    first_half = values[..., :half_rot]
    second_half = values[..., half_rot : 2 * half_rot]
    remain = values[..., 2 * half_rot :]
    return jnp.concatenate(
        [
            first_half * cosine + second_half * sine_tab,
            second_half * cosine - first_half * sine_tab,
            remain,
        ],
        axis=-1,
    )


def gelu_tanh(values):
    return jax.nn.gelu(values, approximate=True)


def contract_rows(left, right):
    return lax.dot_general(
        left, right, (((0,), (0,)), ((), ())), preferred_element_type=jnp.float32
    )


def contract_cols(left, right):
    return lax.dot_general(
        left, right, (((1,), (1,)), ((), ())), preferred_element_type=jnp.float32
    )


def masked_scores(query_blk, keys_rot, doc_query, doc_rows, query_index, key_index, factor):
    scores = (
        jnp.einsum("hqd,hkd->hqk", query_blk, keys_rot, preferred_element_type=jnp.float32) * factor
    )
    allowed = (doc_query[:, None] == doc_rows[None, :]) & (
        key_index[None, :] <= query_index[:, None]
    )
    return jnp.where(allowed[None], scores, NEGATIVE)


def local(
    tokens,
    doc_ids,
    real_rows,
    cotangent,
    norm_gain,
    norm_shift,
    out_bias,
    w_qkv,
    b_qkv,
    w_out,
    w_up,
    b_up,
    w_down,
):
    member = lax.axis_index("branch")
    my_rows = tokens.shape[0]
    broadcast_gain, broadcast_shift, bias_full = (
        lax.all_gather(norm_gain.astype(jnp.bfloat16), ("dp", "branch"), axis=0, tiled=True),
        lax.all_gather(norm_shift.astype(jnp.bfloat16), ("dp", "branch"), axis=0, tiled=True),
        lax.all_gather(out_bias.astype(jnp.bfloat16), ("dp", "branch"), axis=0, tiled=True),
    )
    broadcast_gain = broadcast_gain.astype(jnp.float32)
    broadcast_shift = broadcast_shift.astype(jnp.float32)
    bias_full = bias_full.astype(jnp.float32)
    xfloat = tokens.astype(jnp.float32)
    mean_removed = xfloat - jnp.mean(xfloat, axis=-1, keepdims=True)
    inverse_deviation = lax.rsqrt(
        jnp.mean(mean_removed * mean_removed, axis=-1, keepdims=True) + NORM_EPS
    )
    standardized_input = mean_removed * inverse_deviation
    normed_input = (standardized_input * broadcast_gain + broadcast_shift).astype(jnp.bfloat16)
    gathered = lax.all_gather(normed_input, "branch", axis=0, tiled=True)
    row_count = gathered.shape[0]
    attn_w, attn_b, out_w = (
        lax.all_gather(w_qkv.astype(jnp.bfloat16), "dp", axis=1, tiled=True),
        lax.all_gather(b_qkv.astype(jnp.bfloat16), "dp", axis=2, tiled=True),
        lax.all_gather(w_out.astype(jnp.bfloat16), "dp", axis=1, tiled=True),
    )
    up_w, up_b, down_w = (
        lax.all_gather(w_up.astype(jnp.bfloat16), "dp", axis=0, tiled=True),
        lax.all_gather(b_up.astype(jnp.bfloat16), "dp", axis=1, tiled=True),
        lax.all_gather(w_down.astype(jnp.bfloat16), "dp", axis=1, tiled=True),
    )
    local_cols = attn_w.shape[2]
    local_heads = local_cols // HEAD_DIM
    project = jnp.einsum("td,cde->cte", gathered, attn_w, preferred_element_type=jnp.float32)
    project = project + attn_b.astype(jnp.float32).reshape(3, 1, local_cols)
    heads_view = project.reshape(3, row_count, local_heads, HEAD_DIM).transpose(0, 2, 1, 3)
    cosine, sine_tab = rotary_tables(doc_ids)
    queries = rotate(heads_view[0], cosine, sine_tab).astype(jnp.bfloat16)
    keys_rot = rotate(heads_view[1], cosine, sine_tab).astype(jnp.bfloat16)
    values_low = heads_view[2].astype(jnp.bfloat16)
    block_rows = min(512, row_count)
    blocks = row_count // block_rows
    row_index = jnp.arange(row_count, dtype=jnp.int32)
    factor = 1.0 / math.sqrt(HEAD_DIM)
    query_blocks = queries.reshape(local_heads, blocks, block_rows, HEAD_DIM).transpose(1, 0, 2, 3)
    doc_blocks = doc_ids.reshape(blocks, block_rows)
    index_blocks = row_index.reshape(blocks, block_rows)

    def forward_block(pieces):
        query_blk, doc_query, query_index = pieces
        masked = masked_scores(
            query_blk, keys_rot, doc_query, doc_ids, query_index, row_index, factor
        )
        row_top = jnp.max(masked, axis=-1, keepdims=True)
        weights_exp = jnp.exp(masked - row_top)
        row_total = jnp.sum(weights_exp, axis=-1, keepdims=True)
        probability = (weights_exp / row_total).astype(jnp.bfloat16)
        result = jnp.einsum(
            "hqk,hkd->hqd", probability, values_low, preferred_element_type=jnp.float32
        )
        return (result.astype(jnp.bfloat16), (row_top + jnp.log(row_total))[..., 0])

    attended, log_total = lax.map(forward_block, (query_blocks, doc_blocks, index_blocks))
    flat_out = attended.transpose(0, 2, 1, 3).reshape(row_count, local_cols)
    hidden_pre = jnp.dot(gathered, up_w, preferred_element_type=jnp.float32) + up_b.astype(
        jnp.float32
    ).reshape(-1)
    activated = gelu_tanh(hidden_pre).astype(jnp.bfloat16)
    partial_value = jnp.dot(flat_out, out_w, preferred_element_type=jnp.float32)
    partial_value = partial_value + jnp.dot(activated, down_w, preferred_element_type=jnp.float32)
    summed = lax.psum_scatter(
        partial_value.astype(jnp.bfloat16), "branch", scatter_dimension=0, tiled=True
    ).astype(jnp.float32)
    my_real = lax.dynamic_slice_in_dim(real_rows, member * my_rows, my_rows).astype(jnp.float32)
    block_out = (xfloat + my_real[:, None] * (summed + bias_full)).astype(jnp.bfloat16)
    masked_cot = (cotangent.astype(jnp.float32) * my_real[:, None]).astype(jnp.bfloat16)
    cot_all = lax.all_gather(masked_cot, "branch", axis=0, tiled=True)
    bias_part = jnp.sum(masked_cot, axis=0, dtype=jnp.float32)
    down_grad = contract_rows(activated, cot_all)
    hidden_grad = contract_cols(cot_all, down_w)
    gelu_value, gelu_pull = jax.vjp(gelu_tanh, hidden_pre)
    pre_grad = gelu_pull(hidden_grad)[0].astype(jnp.bfloat16)
    up_grad = contract_rows(gathered, pre_grad)
    up_bias_grad = jnp.sum(pre_grad, axis=0, dtype=jnp.float32).reshape(up_b.shape)
    normed_grad = contract_cols(pre_grad, up_w)
    out_grad_w = contract_rows(flat_out, cot_all)
    flat_dout = contract_cols(cot_all, out_w).astype(jnp.bfloat16)
    dout_blocks = flat_dout.reshape(blocks, block_rows, local_heads, HEAD_DIM).transpose(0, 2, 1, 3)

    def backward_block(running_acc, pieces):
        key_acc, value_acc = running_acc
        query_blk, dout_blk, log_blk, doc_query, query_index = pieces
        masked = masked_scores(
            query_blk, keys_rot, doc_query, doc_ids, query_index, row_index, factor
        )
        probability = jnp.exp(masked - log_blk[..., None])
        value_acc = value_acc + jnp.einsum(
            "hqk,hqd->hkd",
            probability.astype(jnp.bfloat16),
            dout_blk,
            preferred_element_type=jnp.float32,
        )
        prob_grad = jnp.einsum(
            "hqd,hkd->hqk", dout_blk, values_low, preferred_element_type=jnp.float32
        )
        score_grad = probability * (
            prob_grad - jnp.sum(probability * prob_grad, axis=-1, keepdims=True)
        )
        score_grad = score_grad.astype(jnp.bfloat16)
        query_grad = (
            jnp.einsum("hqk,hkd->hqd", score_grad, keys_rot, preferred_element_type=jnp.float32)
            * factor
        )
        key_acc = (
            key_acc
            + jnp.einsum("hqk,hqd->hkd", score_grad, query_blk, preferred_element_type=jnp.float32)
            * factor
        )
        return ((key_acc, value_acc), query_grad)

    zero_acc = jnp.zeros((local_heads, row_count, HEAD_DIM), jnp.float32)
    (key_grad, value_grad), query_grads = lax.scan(
        backward_block,
        (zero_acc, zero_acc),
        (query_blocks, dout_blocks, log_total, doc_blocks, index_blocks),
    )
    query_grad = query_grads.transpose(1, 0, 2, 3).reshape(local_heads, row_count, HEAD_DIM)
    stacked = jnp.stack(
        [unrotate(query_grad, cosine, sine_tab), unrotate(key_grad, cosine, sine_tab), value_grad]
    )
    qkv_grad = stacked.transpose(0, 2, 1, 3).reshape(3, row_count, local_cols).astype(jnp.bfloat16)
    attn_grad_w = jnp.einsum("td,cte->cde", gathered, qkv_grad, preferred_element_type=jnp.float32)
    attn_bias_grad = jnp.sum(qkv_grad, axis=1, dtype=jnp.float32).reshape(attn_b.shape)
    normed_grad = normed_grad + jnp.einsum(
        "cte,cde->td", qkv_grad, attn_w, preferred_element_type=jnp.float32
    )
    w_qkv_grad, b_qkv_grad, w_out_grad, w_up_grad, b_up_grad, w_down_grad = (
        lax.psum_scatter(
            attn_grad_w.astype(jnp.bfloat16), "dp", scatter_dimension=1, tiled=True
        ).astype(jnp.float32),
        lax.psum_scatter(
            attn_bias_grad.astype(jnp.bfloat16), "dp", scatter_dimension=2, tiled=True
        ).astype(jnp.float32),
        lax.psum_scatter(
            out_grad_w.astype(jnp.bfloat16), "dp", scatter_dimension=1, tiled=True
        ).astype(jnp.float32),
        lax.psum_scatter(
            up_grad.astype(jnp.bfloat16), "dp", scatter_dimension=0, tiled=True
        ).astype(jnp.float32),
        lax.psum_scatter(
            up_bias_grad.astype(jnp.bfloat16), "dp", scatter_dimension=1, tiled=True
        ).astype(jnp.float32),
        lax.psum_scatter(
            down_grad.astype(jnp.bfloat16), "dp", scatter_dimension=1, tiled=True
        ).astype(jnp.float32),
    )
    normed_total_sum = lax.psum_scatter(
        normed_grad.astype(jnp.bfloat16), "branch", scatter_dimension=0, tiled=True
    ).astype(jnp.float32)
    scaled_input = normed_total_sum * broadcast_gain
    input_grad = inverse_deviation * (
        scaled_input
        - jnp.mean(scaled_input, axis=-1, keepdims=True)
        - standardized_input * jnp.mean(scaled_input * standardized_input, axis=-1, keepdims=True)
    )
    tokens_grad = (cotangent.astype(jnp.float32) + input_grad).astype(jnp.bfloat16)
    gain_sums, shift_sums, bias_sums = (
        lax.psum_scatter(
            jnp.sum(normed_total_sum * standardized_input, axis=0),
            ("dp", "branch"),
            scatter_dimension=0,
            tiled=True,
        ),
        lax.psum_scatter(
            jnp.sum(normed_total_sum, axis=0), ("dp", "branch"), scatter_dimension=0, tiled=True
        ),
        lax.psum_scatter(bias_part, ("dp", "branch"), scatter_dimension=0, tiled=True),
    )
    return (
        block_out,
        tokens_grad,
        gain_sums,
        shift_sums,
        bias_sums,
        w_qkv_grad,
        b_qkv_grad,
        w_out_grad,
        w_up_grad,
        b_up_grad,
        w_down_grad,
    )


def solution(mesh):
    in_specs = (
        P(("dp", "branch"), None),
        P("dp"),
        P("dp"),
        P(("dp", "branch"), None),
        P(("dp", "branch")),
        P(("dp", "branch")),
        P(("dp", "branch")),
        P(None, "dp", "branch"),
        P(None, "branch", "dp"),
        P("branch", "dp"),
        P("dp", "branch"),
        P("branch", "dp"),
        P("branch", "dp"),
    )
    out_specs = (
        P(("dp", "branch"), None),
        P(("dp", "branch"), None),
        P(("dp", "branch")),
        P(("dp", "branch")),
        P(("dp", "branch")),
        P(None, "dp", "branch"),
        P(None, "branch", "dp"),
        P("branch", "dp"),
        P("dp", "branch"),
        P("branch", "dp"),
        P("branch", "dp"),
    )
    return jax.shard_map(local, mesh=mesh, in_specs=in_specs, out_specs=out_specs, check_vma=False)
```

profile of v0, /device:TPU:0, one launch (start us, length us, event | category | flops | bytes accessed | tf_op | source)
XLA Modules:
  0.0 864.9 jit_solution(15730923838003511770)
XLA Ops:
  14.5 42.2 %all-reduce.8 = (bf16[2048]{0:T(1024)(128)(2,1)S(1)}, bf16[2048]{0:T(1024)(128)(2,1)S(1)}, bf16[2048]{0:T(1024)(128)(2,1)}) all-reduce(bf16[2048]{0:T(1024)(128)(2,1)S(1)} %dynamic-update-slice.1, bf16[2048]{0:T(1024)(128)(2,1)S(1)} %dynamic-update-slice, ...), channel_id=1, replica_groups=mesh['dp'=8,'branch'=4] {'dp','branch'}, use_global_device_ids=true, to_apply=%add.1 | all-reduce | flops 6144 | bytes 24576
  66.5 10.4 %all_gather.37 = bf16[3,8,64]{1,0,2:T(4,128)(2,1)S(1)} all-gather(bf16[3,8,8]{1,0,2:T(4,128)(2,1)S(1)} %copy.73), channel_id=1, replica_groups=mesh['dp'=8,'branch'=4] {'dp'}, dimensions={2}, use_global_device_ids=true | all-gather | bytes 3456 | tf_op jit(solution)/shard_map/all_gather | solution.py:121
  87.0 37.6 %all-gather.17.cloned.1.call-done = bf16[1024,2048]{1,0:T(8,128)(2,1)} async-done(((bf16[256,2048]{1,0:T(8,128)(2,1)}), bf16[1024,2048]{1,0:T(8,128)(2,1)}) %all-gather.17.cloned.1.call-update) | async-done | bytes 4194320 | tf_op jit(solution)/shard_map/all_gather | solution.py:174
  132.8 73.2 %all-gather.7.cloned.1.call-done = bf16[1024,2048]{1,0:T(8,128)(2,1)} async-done(((bf16[256,2048]{1,0:T(8,128)(2,1)}), bf16[1024,2048]{1,0:T(8,128)(2,1)}) %all-gather.7.cloned.1.call-update) | async-done | bytes 4194320 | tf_op jit(solution)/shard_map/all_gather | solution.py:117
  206.0 47.0 %all-gather.9.cloned.1.call-done = bf16[3,2048,512]{1,2,0:T(8,128)(2,1)} async-done(((bf16[3,256,512]{1,2,0:T(8,128)(2,1)}), bf16[3,2048,512]{1,2,0:T(8,128)(2,1)}) %all-gather.9.cloned.1.call-update) | async-done | bytes 6291472 | tf_op jit(solution)/shard_map/all_gather | solution.py:120
  266.6 31.2 %while.28 = (s32[]{:T(128)}, bf16[2,8,512,64]{2,3,1,0:T(8,128)(2,1)S(1)}, f32[2,8,512]{2,1,0:T(8,128)}, s32[2,512]{1,0:T(2,128)S(1)}, s32[1024]{0:T(1024)S(1)}, ...) while((s32[]{:T(128)}, ...), condition=%wide.region_7.8_spmd.clone, body=%wide.region_4.7_spmd.clone.sunk | while | flops 1125904384 | bytes 55723116 | solution.py:160
  298.7 96.8 %while.29 = (s32[]{:T(128)}, f32[8,1024,64]{1,2,0:T(8,128)}, f32[8,1024,64]{1,2,0:T(8,128)}, f32[2,8,512,64]{2,3,1,0:T(8,128)}, s32[2,512]{1,0:T(2,128)S(1)}, /*...) while((s32[]{:T(128)}, f32[8,1024,64]{1,2,0:T(8,128)}, ...), condition=%wide.region_11.12_spmd.clone, body=%wide.region_9.11_spmd.clone.sunk | while | flops 2726555648 | bytes 229869888 | solution.py:219
  304.7 11.4 %multiply_reduce_fusion.2 = (f32[8,512]{1,0:T(8,128)}, f32[8,512,1024]{2,1,0:T(8,128)}) fusion(f32[8,512,1024]{2,1,0:T(8,128)S(1)} %fusion.136, f32[8,512]{1,0:T(8,128)} %dynamic-slice_bitcast_fusion.2, bf16[8,1024,64]{1,2,0:T(8,128)(2,1)S(1)} %get-tuple-element.598, bf16[2,8,512,64]{2,3,1,0:T(8,128)(2,1)} %get-tuple-element.597, ...), kind=kOutput, calls=%fused_computation.23.clone.1 | convolution fusion | flops 557838336 | bytes 35684864 | tf_op jit(solution)/shard_map/while/body/eval_jaxpr/hqd,hkd->hqk/dot_general | solution.py:77
  316.1 10.9 %multiply_convert_fusion.5 = bf16[8,512,1024]{2,1,0:T(8,128)(2,1)} fusion(f32[8,512,1024]{2,1,0:T(8,128)} %get-tuple-element.530, f32[8,512,1024]{2,1,0:T(8,128)S(1)} %fusion.136, f32[8,512]{1,0:T(8,128)} %get-tuple-element.531), kind=kLoop, calls=%fused_computation.22.clone.1 | loop fusion | flops 12582912 | bytes 41959424 | tf_op jit(solution)/shard_map/while/body/eval_jaxpr/convert_element_type | solution.py:206
  353.2 11.5 %multiply_reduce_fusion.2 = (f32[8,512]{1,0:T(8,128)}, f32[8,512,1024]{2,1,0:T(8,128)}) fusion(f32[8,512,1024]{2,1,0:T(8,128)S(1)} %fusion.136, f32[8,512]{1,0:T(8,128)} %dynamic-slice_bitcast_fusion.2, bf16[8,1024,64]{1,2,0:T(8,128)(2,1)S(1)} %get-tuple-element.598, bf16[2,8,512,64]{2,3,1,0:T(8,128)(2,1)} %get-tuple-element.597, ...), kind=kOutput, calls=%fused_computation.23.clone.1 | convolution fusion | flops 557838336 | bytes 35684864 | tf_op jit(solution)/shard_map/while/body/eval_jaxpr/hqd,hkd->hqk/dot_general | solution.py:77
  406.7 14.7 %fusion.74 = f32[1024,2048]{1,0:T(8,128)} fusion(bf16[1024,2048]{1,0:T(8,128)(2,1)} %all-gather.7.cloned.1.call-done, bf16[2048,2048]{1,0:T(8,128)(2,1)} %all-gather.13.cloned.1.call-done), kind=kOutput, calls=%fused_computation.140 | convolution fusion | flops 8589934592 | bytes 20971520 | tf_op jit(solution)/shard_map/dot_general | solution.py:162
  421.4 20.3 %fusion.70 = (bf16[2048]{0:T(1024)(128)(2,1)S(1)}, bf16[1024,2048]{1,0:T(8,128)(2,1)}) fusion(f32[1024,2048]{1,0:T(8,128)} %fusion.74, f32[2048]{0:T(1024)S(1)} %copy-done.32, bf16[1024,2048]{1,0:T(8,128)(2,1)} %all-gather.17.cloned.1.call-done, bf16[2048,2048]{1,0:T(8,128)(2,1)} %all-gather.15.cloned.1.call-done), kind=kOutput, calls=%fused_computation.138 | convolution fusion | flops 8636069888 | bytes 25178112 | tf_op jit(solution)/shard_map/dot_general | solution.py:70
  442.5 11.2 %convert_bitcast_fusion = bf16[3,2048,512]{1,2,0:T(8,128)(2,1)} fusion(bf16[3,1024,512]{1,2,0:T(8,128)(2,1)S(1)} %bitcast.179, bf16[1024,2048]{1,0:T(8,128)(2,1)} %all-gather.7.cloned.1.call-done), kind=kOutput, calls=%fused_computation.66 | convolution fusion | flops 6445596672 | bytes 13631488 | tf_op jit(solution)/shard_map/td,cte->cde/dot_general | solution.py:229
  453.8 12.6 %fusion.75 = f32[1024,2048]{1,0:T(8,128)S(1)} fusion(bf16[1024,2048]{1,0:T(8,128)(2,1)} %get-tuple-element.355, bf16[2048,2048]{1,0:T(8,128)(2,1)} %all-gather.13.cloned.1.call-done), kind=kOutput, calls=%fused_computation.141 | convolution fusion | flops 8589934592 | bytes 20971520 | tf_op jit(solution)/shard_map/dot_general | solution.py:70
  466.4 11.2 %fusion.44 = bf16[1024,2048]{1,0:T(8,128)(2,1)} fusion(f32[1024,2048]{1,0:T(8,128)S(1)} %fusion.75, bf16[3,1024,512]{1,2,0:T(8,128)(2,1)S(1)} %bitcast.180, bf16[3,2048,512]{1,2,0:T(8,128)(2,1)} %all-gather.9.cloned.1.call-done), kind=kOutput, calls=%fused_computation.60 | convolution fusion | flops 6446645248 | bytes 22020096 | tf_op jit(solution)/shard_map/cte,cde->td/dot_general | solution.py:231
  477.7 15.8 %fusion.69 = f32[1024,2048]{1,0:T(8,128)S(1)} fusion(bf16[2048,2048]{1,0:T(8,128)(2,1)} %all-gather.15.cloned.1.call-done, f32[1024,2048]{1,0:T(8,128)} %fusion.74, f32[2048]{0:T(1024)S(1)} %copy-done.32), kind=kOutput, calls=%fused_computation.137 | convolution fusion | flops 8610906112 | bytes 25174016 | tf_op jit(solution)/shard_map/dot_general | solution.py:167
  497.9 14.2 %convolution_convert_fusion.1 = bf16[2048,2048]{1,0:T(8,128)(2,1)} fusion(bf16[1024,2048]{1,0:T(8,128)(2,1)} %all-gather.7.cloned.1.call-done, bf16[1024,2048]{1,0:T(8,128)(2,1)} %get-tuple-element.355), kind=kOutput, calls=%fused_computation.64 | convolution fusion | flops 8594128896 | bytes 16777216 | tf_op jit(solution)/shard_map/dot_general | solution.py:64
  512.2 16.2 %convolution_convert_fusion = bf16[2048,2048]{1,0:T(8,128)(2,1)} fusion(bf16[1024,2048]{1,0:T(8,128)(2,1)} %all-gather.17.cloned.1.call-done, f32[1024,2048]{1,0:T(8,128)} %fusion.74, f32[2048]{0:T(1024)S(1)} %copy-done.32), kind=kOutput, calls=%fused_computation.63 | convolution fusion | flops 8615100416 | bytes 20979712 | tf_op jit(solution)/shard_map/dot_general | solution.py:64
  530.3 12.9 %all-reduce.6 = bf16[3,8,64]{2,1,0:T(8,128)(2,1)S(1)} all-reduce(bf16[3,8,64]{2,1,0:T(8,128)(2,1)S(1)} %copy-done.25), channel_id=8, replica_groups=mesh['dp'=8,'branch'=4] {'dp'}, use_global_device_ids=true, to_apply=%region_23.24.clone | all-reduce | flops 1536 | bytes 6144
  549.6 74.9 %reduce-scatter.13.cloned.1.call-done = bf16[256,2048]{1,0:T(8,128)(2,1)} async-done(((bf16[1024,2048]{1,0:T(8,128)(2,1)}), bf16[256,2048]{1,0:T(8,128)(2,1)}) %reduce-scatter.13.cloned.1.call-update) | async-done | bytes 1048592 | tf_op jit(solution)/shard_map/reduce_scatter | solution.py:254
  626.8 46.3 %all-reduce.7 = (f32[2048]{0:T(1024)S(1)}, f32[2048]{0:T(1024)S(1)}, f32[2048]{0:T(1024)S(1)}) all-reduce(f32[2048]{0:T(1024)S(1)} %get-tuple-element.302, f32[2048]{0:T(1024)S(1)} %get-tuple-element.305, f32[2048]{0:T(1024)S(1)} %copy-done.22), channel_id=4, replica_groups=mesh['dp'=8,'branch'=4] {'dp','branch'}, use_global_device_ids=true, to_apply=%region_16.17.clone | all-reduce | flops 6144 | bytes 49152
  674.8 30.3 %reduce-scatter.11.cloned.1.call-done = bf16[256,2048]{1,0:T(8,128)(2,1)} async-done(((bf16[1024,2048]{1,0:T(8,128)(2,1)}), bf16[256,2048]{1,0:T(8,128)(2,1)}) %reduce-scatter.11.cloned.1.call-update) | async-done | bytes 1048592 | tf_op jit(solution)/shard_map/reduce_scatter | solution.py:168
  709.1 71.5 %reduce-scatter.19.cloned.1.call-done = bf16[256,2048]{1,0:T(8,128)(2,1)} async-done(((bf16[2048,2048]{1,0:T(8,128)(2,1)}), bf16[256,2048]{1,0:T(8,128)(2,1)}) %reduce-scatter.19.cloned.1.call-update) | async-done | bytes 1048592 | tf_op jit(solution)/shard_map/reduce_scatter | solution.py:244
  783.5 72.0 %reduce-scatter.21.cloned.1.call-done = bf16[2048,256]{1,0:T(8,128)(2,1)} async-done(((bf16[2048,2048]{1,0:T(8,128)(2,1)}), bf16[2048,256]{1,0:T(8,128)(2,1)}) %reduce-scatter.21.cloned.1.call-update) | async-done | bytes 1048592 | tf_op jit(solution)/shard_map/reduce_scatter | solution.py:250
  (237 shorter events, 180.7 us)
Async XLA Ops:
  7.2 49.4 %copy-start.5 = (bf16[256,2048]{1,0:T(8,128)(2,1)S(1)}, bf16[256,2048]{1,0:T(8,128)(2,1)}, u32[]{:S(2)}) copy-start(bf16[256,2048]{1,0:T(8,128)(2,1)} %param.17) | copy-start | bytes 3145732
  7.2 79.7 %all-gather.11.cloned.1.call-start = ((), (), s32[]{:S(2)}) async-start(), calls=%async_computation.9 | async-start | bytes 2359296 | tf_op jit(solution)/shard_map/all_gather | solution.py:122
  9.1 115.4 %all-gather.17.cloned.1.call-start = ((), (), s32[]{:S(2)}) async-start(), calls=%async_computation.13 | async-start | bytes 5242880 | tf_op jit(solution)/shard_map/all_gather | solution.py:174
  13.6 192.4 %all-gather.7.cloned.1.call-start = ((), (), s32[]{:S(2)}) async-start(), calls=%async_computation.7 | async-start | bytes 5242880 | tf_op jit(solution)/shard_map/all_gather | solution.py:117
  59.5 193.5 %all-gather.9.cloned.1.call-start = ((), (), s32[]{:S(2)}) async-start(), calls=%async_computation.8 | async-start | bytes 7077888 | tf_op jit(solution)/shard_map/all_gather | solution.py:120
  62.3 344.5 %all-gather.13.cloned.1.call-start = ((), (), s32[]{:S(2)}) async-start(), calls=%async_computation.10 | async-start | bytes 9437184 | tf_op jit(solution)/shard_map/all_gather | solution.py:125
  63.5 358.0 %all-gather.15.cloned.1.call-start = ((), (), s32[]{:S(2)}) async-start(), calls=%async_computation.11 | async-start | bytes 9437184 | tf_op jit(solution)/shard_map/all_gather | solution.py:127
  66.2 477.7 %reduce-scatter.17.cloned.1.call-start = ((), (), s32[]{:S(2)}) async-start(), calls=%async_computation.16 | async-start | bytes 2359296 | tf_op jit(solution)/shard_map/reduce_scatter | solution.py:241
  86.9 178.1 %copy-start.15 = (f32[1024,16]{0,1:T(8,128)}, f32[1024,16]{0,1:T(8,128)S(1)}, u32[]{:S(2)}) copy-start(f32[1024,16]{0,1:T(8,128)S(1)} %get-tuple-element.384) | copy-start | bytes 196612
  86.9 178.1 %copy-start.17 = (f32[1024,16]{0,1:T(8,128)}, f32[1024,16]{0,1:T(8,128)S(1)}, u32[]{:S(2)}) copy-start(f32[1024,16]{0,1:T(8,128)S(1)} %get-tuple-element.385) | copy-start | bytes 196612
  404.1 141.6 %reduce-scatter.23.cloned.1.call-start = ((), (), s32[]{:S(2)}) async-start(), calls=%async_computation.19 | async-start | bytes 36864
  442.5 104.5 %reduce-scatter.15.cloned.1.call-start = ((), (), s32[]{:S(2)}) async-start(), calls=%async_computation.15 | async-start | bytes 7077888 | tf_op jit(solution)/shard_map/reduce_scatter | solution.py:235
  453.7 170.7 %reduce-scatter.13.cloned.1.call-start = ((), (), s32[]{:S(2)}) async-start(), calls=%async_computation.14 | async-start | bytes 5242880 | tf_op jit(solution)/shard_map/reduce_scatter | solution.py:254
  477.6 15.9 %copy-start.13 = (bf16[64,8,2,512]{3,1,2,0:T(8,128)(2,1)S(1)}, bf16[64,8,2,512]{3,1,2,0:T(8,128)(2,1)}, u32[]{:S(2)}) copy-start(bf16[64,8,2,512]{3,1,2,0:T(8,128)(2,1)} %copy-done.12) | copy-start | bytes 3145732
  477.6 227.5 %reduce-scatter.11.cloned.1.call-start = ((), (), s32[]{:S(2)}) async-start(), calls=%async_computation.12 | async-start | bytes 5242880 | tf_op jit(solution)/shard_map/reduce_scatter | solution.py:168
  497.9 282.8 %reduce-scatter.19.cloned.1.call-start = ((), (), s32[]{:S(2)}) async-start(), calls=%async_computation.17 | async-start | bytes 9437184 | tf_op jit(solution)/shard_map/reduce_scatter | solution.py:244
  512.1 343.3 %reduce-scatter.21.cloned.1.call-start = ((), (), s32[]{:S(2)}) async-start(), calls=%async_computation.18 | async-start | bytes 9437184 | tf_op jit(solution)/shard_map/reduce_scatter | solution.py:250
  528.4 96.1 %copy-start.6 = (bf16[256,2048]{1,0:T(8,128)(2,1)S(1)}, bf16[256,2048]{1,0:T(8,128)(2,1)}, u32[]{:S(2)}) copy-start(bf16[256,2048]{1,0:T(8,128)(2,1)} %param.17) | copy-start | bytes 3145732
  528.4 96.1 %copy-start.21 = (f32[2048]{0:T(1024)S(1)}, f32[2048]{0:T(1024)}, u32[]{:S(2)}) copy-start(f32[2048]{0:T(1024)} %copy-done.20) | copy-start | bytes 24580
  528.4 96.0 %copy-start.24 = (f32[256]{0:T(256)S(1)}, f32[256]{0:T(256)}, u32[]{:S(2)}) copy-start(f32[256]{0:T(256)} %copy-done.23) | copy-start | bytes 3076
  528.4 96.0 %copy-start.27 = (f32[256]{0:T(256)S(1)}, f32[256]{0:T(256)}, u32[]{:S(2)}) copy-start(f32[256]{0:T(256)} %copy-done.26) | copy-start | bytes 3076
  528.5 98.3 %copy-start.22 = (f32[2048]{0:T(1024)S(1)}, f32[2048]{0:T(1024)}, u32[]{:S(2)}) copy-start(f32[2048]{0:T(1024)} %get-tuple-element.358) | copy-start | bytes 24580
  528.5 176.6 %copy-start.7 = (bf16[256,2048]{1,0:T(8,128)(2,1)S(1)}, bf16[256,2048]{1,0:T(8,128)(2,1)}, u32[]{:S(2)}) copy-start(bf16[256,2048]{1,0:T(8,128)(2,1)} %param.20) | copy-start | bytes 3145732
  528.5 176.6 %copy-start.30 = (f32[256]{0:T(256)S(1)}, f32[256]{0:T(256)}, u32[]{:S(2)}) copy-start(f32[256]{0:T(256)} %copy-done.29) | copy-start | bytes 3076
  (34 other events, 176.7 us)
Sparse Core Ops, SparseCore 0:
  10.5 31.0 all-gather.10
  43.8 80.7 all-gather.16
  126.7 79.2 all-gather.6
  207.8 45.1 all-gather.8
  255.3 54.4 all-gather.12
  311.5 55.9 all-gather.14
  404.2 40.4 reduce-scatter.16
  448.5 31.2 reduce-scatter.22
  483.2 62.1 reduce-scatter.14
  547.6 76.8 reduce-scatter.12
  626.8 78.2 reduce-scatter.10
  708.8 71.8 reduce-scatter.18
  784.1 71.2 reduce-scatter.20
where the time goes:
time: 872 us; the launch traced here: 865 us
  waiting for transfers between devices  407 us (47%)
  matrix products  223 us (26%)
  blocking collectives  120 us (14%)
  other arithmetic  66.4 us (8%)
  local copies, waits for them, and re-layouts  32.5 us (4%)
  between operations  15.5 us (2%)
    unnamed x3, blocking collectives  101 us
    reduce_scatter x1, waiting for transfers between devices, local(): lax.psum_scatter(normed_grad.astype(jnp.bfloat16), 'branch', scatter_dime...  74.9 us
    all_gather x1, waiting for transfers between devices, local(): gathered = lax.all_gather(normed_input, 'branch', axis=0, tiled=True)  73.2 us
    reduce_scatter x1, waiting for transfers between devices, local(): lax.psum_scatter(down_grad.astype(jnp.bfloat16), 'dp', scatter_dimension=...  72 us
    reduce_scatter x1, waiting for transfers between devices, local(): lax.psum_scatter(up_grad.astype(jnp.bfloat16), 'dp', scatter_dimension=0,...  71.5 us
    all_gather x1, waiting for transfers between devices, local(): lax.all_gather(w_qkv.astype(jnp.bfloat16), 'dp', axis=1, tiled=True)  47 us
    dot_general x3, matrix products, contract_cols(): lax.dot_general(left, right, (((1,), (1,)), ((), ())), preferred_element_...  38.1 us
    all_gather x1, waiting for transfers between devices, local(): cot_all = lax.all_gather(masked_cot, 'branch', axis=0, tiled=True)  37.6 us
  transfers between devices with their start and end apart: 13, of which 7 were waited for; matrix products, arithmetic and copies ran while one was open for 35% of the time, Pallas kernels for 0%

commit v1 on v0

--- a/solution.py
+++ b/solution.py
@@ -171,7 +171,14 @@
     my_real = lax.dynamic_slice_in_dim(real_rows, member * my_rows, my_rows).astype(jnp.float32)
     block_out = (xfloat + my_real[:, None] * (summed + bias_full)).astype(jnp.bfloat16)
     masked_cot = (cotangent.astype(jnp.float32) * my_real[:, None]).astype(jnp.bfloat16)
-    cot_all = lax.all_gather(masked_cot, "branch", axis=0, tiled=True)
+    ring = [masked_cot]
+    for hop in range(3):
+        ring.append(lax.ppermute(ring[-1], "branch", [(dev, (dev + 1) % 4) for dev in range(4)]))
+    cot_all = jnp.roll(
+        jnp.concatenate(ring[::-1], axis=0),
+        (lax.axis_index("branch") + 1) * ring[0].shape[0],
+        axis=0,
+    )
     bias_part = jnp.sum(masked_cot, axis=0, dtype=jnp.float32)
     down_grad = contract_rows(activated, cot_all)
     hidden_grad = contract_cols(cot_all, down_w)

time: 872 us -> 856 us (0.982)
  waiting for transfers between devices: 407 us -> 342 us
  starting transfers between devices: 0.54 us -> 26.6 us
  local copies, waits for them, and re-layouts: 32.5 us -> 44.8 us
    ppermute x0 -> x3, waiting for transfers between devices: none -> 90.4 us  [local(): lax.ppermute(ring[-1], 'branch', [(dev, (dev + 1) % 4) for dev in range(4)])]
    all_gather x1, waiting for transfers between devices: 73.2 us -> 0.01 us  [local(): gathered = lax.all_gather(normed_input, 'branch', axis=0, tiled=True)]
    all_gather x1, waiting for transfers between devices: 47 us -> 5.43 us  [local(): lax.all_gather(w_qkv.astype(jnp.bfloat16), 'dp', axis=1, tiled=True)]
    all_gather x1 -> x0, waiting for transfers between devices: 37.6 us -> none  [local(): cot_all = lax.all_gather(masked_cot, 'branch', axis=0, tiled=True)]
    ppermute x0 -> x3, starting transfers between devices: none -> 26.1 us  [local(): lax.ppermute(ring[-1], 'branch', [(dev, (dev + 1) % 4) for dev in range(4)])]
    unnamed x87 -> x80, local copies, waits for them, and re-layouts: 15.2 us -> 23.4 us
  transfers between devices with their start and end apart: 13 -> 15, of which waited for: 7 -> 8; matrix products, arithmetic and copies ran while one was open for 35% -> 39% of each run, Pallas kernels for 0% -> 0%
where the time goes in v1:
time: 856 us; the launch traced here: 848 us
  waiting for transfers between devices  342 us (40%)
  matrix products  228 us (27%)
  blocking collectives  121 us (14%)
  other arithmetic  70.2 us (8%)
  local copies, waits for them, and re-layouts  44.8 us (5%)
  starting transfers between devices  26.6 us (3%)
  between operations  15.7 us (2%)
    unnamed x3, blocking collectives  103 us
    ppermute x3, waiting for transfers between devices, local(): lax.ppermute(ring[-1], 'branch', [(dev, (dev + 1) % 4) for dev in range(4)])  90.4 us
    reduce_scatter x1, waiting for transfers between devices, local(): lax.psum_scatter(up_grad.astype(jnp.bfloat16), 'dp', scatter_dimension=0,...  72 us
    reduce_scatter x1, waiting for transfers between devices, local(): lax.psum_scatter(down_grad.astype(jnp.bfloat16), 'dp', scatter_dimension=...  71.7 us
    reduce_scatter x1, waiting for transfers between devices, local(): lax.psum_scatter(normed_grad.astype(jnp.bfloat16), 'branch', scatter_dime...  71.5 us
    dot_general x3, matrix products, contract_rows(): lax.dot_general(left, right, (((0,), (0,)), ((), ())), preferred_element_...  39.7 us
    dot_general x3, matrix products, contract_cols(): lax.dot_general(left, right, (((1,), (1,)), ((), ())), preferred_element_...  37.7 us
    dot_general x4, matrix products, masked_scores(): jnp.einsum('hqd,hkd->hqk', query_blk, keys_rot, preferred_element_type=jn...  31.4 us
  transfers between devices with their start and end apart: 15, of which 8 were waited for; matrix products, arithmetic and copies ran while one was open for 39% of the time, Pallas kernels for 0%

profile of v1, /device:TPU:0, one launch (start us, length us, event | category | flops | bytes accessed | tf_op | source)
XLA Modules:
  0.0 848.1 jit_solution(3398362626419408266)
XLA Ops:
  11.7 42.1 %all-reduce.8 = (bf16[2048]{0:T(1024)(128)(2,1)S(1)}, bf16[2048]{0:T(1024)(128)(2,1)S(1)}, bf16[2048]{0:T(1024)(128)(2,1)}) all-reduce(bf16[2048]{0:T(1024)(128)(2,1)S(1)} %dynamic-update-slice.1, bf16[2048]{0:T(1024)(128)(2,1)S(1)} %dynamic-update-slice, ...), channel_id=1, replica_groups=mesh['dp'=8,'branch'=4] {'dp','branch'}, use_global_device_ids=true, to_apply=%add.1 | all-reduce | flops 6144 | bytes 24576
  69.1 46.6 %collective-permute-done = bf16[256,2048]{1,0:T(8,128)(2,1)S(1)} collective-permute-done((bf16[256,2048]{1,0:T(8,128)(2,1)S(1)}, bf16[256,2048]{1,0:T(8,128)(2,1)S(1)}, u32[]{:S(2)}, u32[]{:S(2)}) %collective-permute-start) | collective-permute-done | bytes 1048608 | tf_op jit(solution)/shard_map/ppermute | solution.py:176
  115.7 22.3 %collective-permute-start.1 = (bf16[256,2048]{1,0:T(8,128)(2,1)S(1)}, bf16[256,2048]{1,0:T(8,128)(2,1)S(1)}, u32[]{:S(2)}, u32[]{:S(2)}) collective-permute-start(bf16[256,2048]{1,0:T(8,128)(2,1)S(1)} %collective-permute-done), channel_id=1, source_target_pairs={{0,1},{1,2},{2,3},{3,0},{4,5},{5,6},{6,7},{7,4},{8,9},{9,10},{10,1... | collective-permute-start | bytes 3145736 | tf_op jit(solution)/shard_map/ppermute | solution.py:176
  140.8 40.7 %collective-permute-done.1 = bf16[256,2048]{1,0:T(8,128)(2,1)S(1)} collective-permute-done((bf16[256,2048]{1,0:T(8,128)(2,1)S(1)}, bf16[256,2048]{1,0:T(8,128)(2,1)S(1)}, u32[]{:S(2)}, u32[]{:S(2)}) %collective-permute-start.1) | collective-permute-done | bytes 1048608 | tf_op jit(solution)/shard_map/ppermute | solution.py:176
  231.4 10.1 %broadcast_add_fusion = f32[1024,3,512]{0,2,1:T(8,128)S(1)} fusion(f32[3,512]{1,0:T(4,128)S(1)} %reshape.336, bf16[3,2048,512]{1,2,0:T(8,128)(2,1)} %all-gather.8.cloned.1.call-done, bf16[1024,2048]{1,0:T(8,128)(2,1)} %all-gather.6.cloned.1.call-done), kind=kOutput, calls=%fused_computation.73 | convolution fusion | flops 6444023808 | bytes 16783360 | tf_op jit(solution)/shard_map/td,cde->cte/dot_general | solution.py:131
  244.9 31.3 %while.28 = (s32[]{:T(128)}, bf16[2,8,512,64]{2,3,1,0:T(8,128)(2,1)S(1)}, f32[2,8,512]{2,1,0:T(8,128)}, s32[2,512]{1,0:T(2,128)S(1)}, s32[1024]{0:T(1024)S(1)}, ...) while((s32[]{:T(128)}, ...), condition=%wide.region_7.8_spmd.clone, body=%wide.region_4.7_spmd.clone.sunk | while | flops 1125904384 | bytes 55723116 | solution.py:160
  278.6 97.0 %while.29 = (s32[]{:T(128)}, f32[8,1024,64]{1,2,0:T(8,128)}, f32[8,1024,64]{1,2,0:T(8,128)}, f32[2,8,512,64]{2,3,1,0:T(8,128)}, s32[2,512]{1,0:T(2,128)S(1)}, /*...) while((s32[]{:T(128)}, f32[8,1024,64]{1,2,0:T(8,128)}, ...), condition=%wide.region_11.12_spmd.clone, body=%wide.region_9.11_spmd.clone.sunk | while | flops 2726555648 | bytes 229738784 | solution.py:226
  285.1 11.5 %multiply_reduce_fusion.2 = (f32[8,512]{1,0:T(8,128)}, f32[8,512,1024]{2,1,0:T(8,128)}) fusion(f32[8,512,1024]{2,1,0:T(8,128)S(1)} %fusion.146, f32[8,512]{1,0:T(8,128)} %dynamic-slice_bitcast_fusion.2, bf16[8,1024,64]{1,2,0:T(8,128)(2,1)S(1)} %get-tuple-element.598, bf16[2,8,512,64]{2,3,1,0:T(8,128)(2,1)} %get-tuple-element.597, ...), kind=kOutput, calls=%fused_computation.23.clone.1 | convolution fusion | flops 557838336 | bytes 35684864 | tf_op jit(solution)/shard_map/while/body/eval_jaxpr/hqd,hkd->hqk/dot_general | solution.py:77
  296.5 9.9 %multiply_convert_fusion.5 = bf16[8,512,1024]{2,1,0:T(8,128)(2,1)} fusion(f32[8,512,1024]{2,1,0:T(8,128)} %get-tuple-element.530, f32[8,512,1024]{2,1,0:T(8,128)S(1)} %fusion.146, f32[8,512]{1,0:T(8,128)} %get-tuple-element.531), kind=kLoop, calls=%fused_computation.22.clone.1 | loop fusion | flops 12582912 | bytes 41959424 | tf_op jit(solution)/shard_map/while/body/eval_jaxpr/convert_element_type | solution.py:213
  333.6 11.5 %multiply_reduce_fusion.2 = (f32[8,512]{1,0:T(8,128)}, f32[8,512,1024]{2,1,0:T(8,128)}) fusion(f32[8,512,1024]{2,1,0:T(8,128)S(1)} %fusion.146, f32[8,512]{1,0:T(8,128)} %dynamic-slice_bitcast_fusion.2, bf16[8,1024,64]{1,2,0:T(8,128)(2,1)S(1)} %get-tuple-element.598, bf16[2,8,512,64]{2,3,1,0:T(8,128)(2,1)} %get-tuple-element.597, ...), kind=kOutput, calls=%fused_computation.23.clone.1 | convolution fusion | flops 557838336 | bytes 35684864 | tf_op jit(solution)/shard_map/while/body/eval_jaxpr/hqd,hkd->hqk/dot_general | solution.py:77
  387.9 14.5 %fusion.88 = f32[1024,2048]{1,0:T(8,128)} fusion(bf16[1024,2048]{1,0:T(8,128)(2,1)} %all-gather.6.cloned.1.call-done, bf16[2048,2048]{1,0:T(8,128)(2,1)} %all-gather.12.cloned.1.call-done), kind=kOutput, calls=%fused_computation.158 | convolution fusion | flops 8589934592 | bytes 20971520 | tf_op jit(solution)/shard_map/dot_general | solution.py:162
  402.4 19.9 %fusion.87 = (bf16[2048]{0:T(1024)(128)(2,1)S(1)}, bf16[1024,2048]{1,0:T(8,128)(2,1)}) fusion(f32[1024,2048]{1,0:T(8,128)} %fusion.88, f32[2048]{0:T(1024)S(1)} %copy-done.28, bf16[2048,2048]{1,0:T(8,128)(2,1)} %all-gather.14.cloned.1.call-done, bf16[2048,2048]{1,0:T(8,128)(2,1)} %constant_dynamic-update-slice_fusion, s32[]{:T(128)S(6)} %select_n.31), kind=kOutput, calls=%fused_computation.157 | convolution fusion | flops 8636069888 | bytes 25178116 | tf_op jit(solution)/shard_map/dot_general | solution.py:70
  423.1 11.1 %convert_bitcast_fusion = bf16[3,2048,512]{1,2,0:T(8,128)(2,1)} fusion(bf16[3,1024,512]{1,2,0:T(8,128)(2,1)S(1)} %bitcast.175, bf16[1024,2048]{1,0:T(8,128)(2,1)} %all-gather.6.cloned.1.call-done), kind=kOutput, calls=%fused_computation.66 | convolution fusion | flops 6445596672 | bytes 13631488 | tf_op jit(solution)/shard_map/td,cte->cde/dot_general | solution.py:236
  434.4 12.6 %fusion.89 = f32[1024,2048]{1,0:T(8,128)S(1)} fusion(bf16[1024,2048]{1,0:T(8,128)(2,1)} %get-tuple-element.385, bf16[2048,2048]{1,0:T(8,128)(2,1)} %all-gather.12.cloned.1.call-done), kind=kOutput, calls=%fused_computation.159 | convolution fusion | flops 8589934592 | bytes 20971520 | tf_op jit(solution)/shard_map/dot_general | solution.py:70
  446.9 11.2 %fusion.44 = bf16[1024,2048]{1,0:T(8,128)(2,1)} fusion(f32[1024,2048]{1,0:T(8,128)S(1)} %fusion.89, bf16[3,1024,512]{1,2,0:T(8,128)(2,1)S(1)} %bitcast.176, bf16[3,2048,512]{1,2,0:T(8,128)(2,1)} %all-gather.8.cloned.1.call-done), kind=kOutput, calls=%fused_computation.60 | convolution fusion | flops 6446645248 | bytes 22020096 | tf_op jit(solution)/shard_map/cte,cde->td/dot_general | solution.py:238
  458.3 15.8 %fusion.84 = f32[1024,2048]{1,0:T(8,128)S(1)} fusion(bf16[2048,2048]{1,0:T(8,128)(2,1)} %all-gather.14.cloned.1.call-done, f32[1024,2048]{1,0:T(8,128)} %fusion.88, f32[2048]{0:T(1024)S(1)} %copy-done.28), kind=kOutput, calls=%fused_computation.155 | convolution fusion | flops 8610906112 | bytes 25174016 | tf_op jit(solution)/shard_map/dot_general | solution.py:167
  478.6 19.8 %convolution_convert_fusion = bf16[2048,2048]{1,0:T(8,128)(2,1)} fusion(bf16[2048,2048]{1,0:T(8,128)(2,1)} %constant_dynamic-update-slice_fusion, s32[]{:T(128)S(6)} %select_n.31, f32[1024,2048]{1,0:T(8,128)} %fusion.88, f32[2048]{0:T(1024)S(1)} %copy-done.28), kind=kOutput, calls=%fused_computation.63 | convolution fusion | flops 8615100416 | bytes 20979716 | tf_op jit(solution)/shard_map/dot_general | solution.py:64
  498.5 14.0 %convolution_convert_fusion.1 = bf16[2048,2048]{1,0:T(8,128)(2,1)} fusion(bf16[1024,2048]{1,0:T(8,128)(2,1)} %all-gather.6.cloned.1.call-done, bf16[1024,2048]{1,0:T(8,128)(2,1)} %get-tuple-element.385), kind=kOutput, calls=%fused_computation.64 | convolution fusion | flops 8594128896 | bytes 16777216 | tf_op jit(solution)/shard_map/dot_general | solution.py:64
  514.5 15.0 %all-reduce.6 = bf16[3,8,64]{2,1,0:T(8,128)(2,1)S(1)} all-reduce(bf16[3,8,64]{2,1,0:T(8,128)(2,1)S(1)} %copy-done.21), channel_id=8, replica_groups=mesh['dp'=8,'branch'=4] {'dp'}, use_global_device_ids=true, to_apply=%region_23.24.clone | all-reduce | flops 1536 | bytes 6144
  535.9 71.5 %reduce-scatter.13.cloned.1.call-done = bf16[256,2048]{1,0:T(8,128)(2,1)} async-done(((bf16[1024,2048]{1,0:T(8,128)(2,1)}), bf16[256,2048]{1,0:T(8,128)(2,1)}) %reduce-scatter.13.cloned.1.call-update) | async-done | bytes 1048592 | tf_op jit(solution)/shard_map/reduce_scatter | solution.py:261
  609.7 46.1 %all-reduce.7 = (f32[2048]{0:T(1024)S(1)}, f32[2048]{0:T(1024)S(1)}, f32[2048]{0:T(1024)S(1)}) all-reduce(f32[2048]{0:T(1024)S(1)} %get-tuple-element.302, f32[2048]{0:T(1024)S(1)} %get-tuple-element.305, f32[2048]{0:T(1024)S(1)} %copy-done.18), channel_id=4, replica_groups=mesh['dp'=8,'branch'=4] {'dp','branch'}, use_global_device_ids=true, to_apply=%region_16.17.clone | all-reduce | flops 6144 | bytes 49152
  657.5 30.4 %reduce-scatter.11.cloned.1.call-done = bf16[256,2048]{1,0:T(8,128)(2,1)} async-done(((bf16[1024,2048]{1,0:T(8,128)(2,1)}), bf16[256,2048]{1,0:T(8,128)(2,1)}) %reduce-scatter.11.cloned.1.call-update) | async-done | bytes 1048592 | tf_op jit(solution)/shard_map/reduce_scatter | solution.py:168
  691.9 71.7 %reduce-scatter.21.cloned.1.call-done = bf16[2048,256]{1,0:T(8,128)(2,1)} async-done(((bf16[2048,2048]{1,0:T(8,128)(2,1)}), bf16[2048,256]{1,0:T(8,128)(2,1)}) %reduce-scatter.21.cloned.1.call-update) | async-done | bytes 1048592 | tf_op jit(solution)/shard_map/reduce_scatter | solution.py:257
  766.3 72.0 %reduce-scatter.19.cloned.1.call-done = bf16[256,2048]{1,0:T(8,128)(2,1)} async-done(((bf16[2048,2048]{1,0:T(8,128)(2,1)}), bf16[256,2048]{1,0:T(8,128)(2,1)}) %reduce-scatter.19.cloned.1.call-update) | async-done | bytes 1048592 | tf_op jit(solution)/shard_map/reduce_scatter | solution.py:251
  (230 shorter events, 211.6 us)
Async XLA Ops:
  7.2 210.4 %all-gather.10.cloned.1.call-start = ((), (), s32[]{:S(2)}) async-start(), calls=%async_computation.9 | async-start | bytes 2359296 | tf_op jit(solution)/shard_map/all_gather | solution.py:122
  9.0 216.9 %all-gather.6.cloned.1.call-start = ((), (), s32[]{:S(2)}) async-start(), calls=%async_computation.7 | async-start | bytes 5242880 | tf_op jit(solution)/shard_map/all_gather | solution.py:117
  60.3 123.5 %copy-start.24 = (f32[3,8,8]{2,1,0:T(8,128)S(1)}, f32[3,8,8]{2,1,0:T(8,128)}, u32[]{:S(2)}) copy-start(f32[3,8,8]{2,1,0:T(8,128)} %param.25) | copy-start | bytes 2308
  60.3 171.1 %all-gather.8.cloned.1.call-start = ((), (), s32[]{:S(2)}) async-start(), calls=%async_computation.8 | async-start | bytes 7077888 | tf_op jit(solution)/shard_map/all_gather | solution.py:120
  62.9 129.4 %copy-start.27 = (f32[16,16]{1,0:T(8,128)S(1)}, f32[16,16]{1,0:T(8,128)}, u32[]{:S(2)}) copy-start(f32[16,16]{1,0:T(8,128)} %param.28) | copy-start | bytes 3076
  63.0 325.0 %all-gather.12.cloned.1.call-start = ((), (), s32[]{:S(2)}) async-start(), calls=%async_computation.10 | async-start | bytes 9437184 | tf_op jit(solution)/shard_map/all_gather | solution.py:125
  65.7 336.7 %all-gather.14.cloned.1.call-start = ((), (), s32[]{:S(2)}) async-start(), calls=%async_computation.11 | async-start | bytes 9437184 | tf_op jit(solution)/shard_map/all_gather | solution.py:127
  66.6 117.2 %copy-start.25 = (f32[256]{0:T(256)}, f32[256]{0:T(256)S(1)}, u32[]{:S(2)}) copy-start(f32[256]{0:T(256)S(1)} %dynamic-slice_convert_fusion.1) | copy-start | bytes 3076
  67.5 48.2 %collective-permute-start = (bf16[256,2048]{1,0:T(8,128)(2,1)S(1)}, bf16[256,2048]{1,0:T(8,128)(2,1)S(1)}, u32[]{:S(2)}, u32[]{:S(2)}) collective-permute-start(bf16[256,2048]{1,0:T(8,128)(2,1)S(1)} %get-tuple-element.357), channel_id=1, source_target_pairs={{0,1},{1,2},{2,3},{3,0},{4,5},{5,6},{6,7},{7,4},{8,9},{9,10},{10,1... | collective-permute-start | bytes 3145736 | tf_op jit(solution)/shard_map/ppermute | solution.py:176
  115.7 65.8 %collective-permute-start.1 = (bf16[256,2048]{1,0:T(8,128)(2,1)S(1)}, bf16[256,2048]{1,0:T(8,128)(2,1)S(1)}, u32[]{:S(2)}, u32[]{:S(2)}) collective-permute-start(bf16[256,2048]{1,0:T(8,128)(2,1)S(1)} %collective-permute-done), channel_id=1, source_target_pairs={{0,1},{1,2},{2,3},{3,0},{4,5},{5,6},{6,7},{7,4},{8,9},{9,10},{10,1... | collective-permute-start | bytes 3145736 | tf_op jit(solution)/shard_map/ppermute | solution.py:176
  140.7 389.5 %reduce-scatter.17.cloned.1.call-start = ((), (), s32[]{:S(2)}) async-start(), calls=%async_computation.15 | async-start | bytes 2359296 | tf_op jit(solution)/shard_map/reduce_scatter | solution.py:248
  181.5 25.0 %collective-permute-start.2 = (bf16[256,2048]{1,0:T(8,128)(2,1)S(1)}, bf16[256,2048]{1,0:T(8,128)(2,1)}, u32[]{:S(2)}, u32[]{:S(2)}) collective-permute-start(bf16[256,2048]{1,0:T(8,128)(2,1)S(1)} %collective-permute-done.1), channel_id=1, source_target_pairs={{0,1},{1,2},{2,3},{3,0},{4,5},{5,6},{6,7},{7,4},{8,9},{9,10},{10,1... | collective-permute-start | bytes 3145736 | tf_op jit(solution)/shard_map/ppermute | solution.py:176
  385.2 146.7 %reduce-scatter.23.cloned.1.call-start = ((), (), s32[]{:S(2)}) async-start(), calls=%async_computation.18 | async-start | bytes 36864
  423.1 110.2 %reduce-scatter.15.cloned.1.call-start = ((), (), s32[]{:S(2)}) async-start(), calls=%async_computation.14 | async-start | bytes 7077888 | tf_op jit(solution)/shard_map/reduce_scatter | solution.py:242
  434.3 173.1 %reduce-scatter.13.cloned.1.call-start = ((), (), s32[]{:S(2)}) async-start(), calls=%async_computation.13 | async-start | bytes 5242880 | tf_op jit(solution)/shard_map/reduce_scatter | solution.py:261
  458.2 229.7 %reduce-scatter.11.cloned.1.call-start = ((), (), s32[]{:S(2)}) async-start(), calls=%async_computation.12 | async-start | bytes 5242880 | tf_op jit(solution)/shard_map/reduce_scatter | solution.py:168
  478.5 285.0 %reduce-scatter.21.cloned.1.call-start = ((), (), s32[]{:S(2)}) async-start(), calls=%async_computation.17 | async-start | bytes 9437184 | tf_op jit(solution)/shard_map/reduce_scatter | solution.py:257
  498.4 339.8 %reduce-scatter.19.cloned.1.call-start = ((), (), s32[]{:S(2)}) async-start(), calls=%async_computation.16 | async-start | bytes 9437184 | tf_op jit(solution)/shard_map/reduce_scatter | solution.py:251
  512.5 94.8 %copy-start.5 = (bf16[256,2048]{1,0:T(8,128)(2,1)S(1)}, bf16[256,2048]{1,0:T(8,128)(2,1)}, u32[]{:S(2)}) copy-start(bf16[256,2048]{1,0:T(8,128)(2,1)} %param.17) | copy-start | bytes 3145732
  512.5 94.8 %copy-start.17 = (f32[2048]{0:T(1024)S(1)}, f32[2048]{0:T(1024)}, u32[]{:S(2)}) copy-start(f32[2048]{0:T(1024)} %copy-done.16) | copy-start | bytes 24580
  512.6 94.8 %copy-start.20 = (f32[256]{0:T(256)S(1)}, f32[256]{0:T(256)}, u32[]{:S(2)}) copy-start(f32[256]{0:T(256)} %copy-done.19) | copy-start | bytes 3076
  512.6 97.1 %copy-start.18 = (f32[2048]{0:T(1024)S(1)}, f32[2048]{0:T(1024)}, u32[]{:S(2)}) copy-start(f32[2048]{0:T(1024)} %get-tuple-element.356) | copy-start | bytes 24580
  512.6 175.3 %copy-start.7 = (bf16[256,2048]{1,0:T(8,128)(2,1)S(1)}, bf16[256,2048]{1,0:T(8,128)(2,1)}, u32[]{:S(2)}) copy-start(bf16[256,2048]{1,0:T(8,128)(2,1)} %param.20) | copy-start | bytes 3145732
  512.6 175.3 %copy-start.26 = (f32[256]{0:T(256)S(1)}, f32[256]{0:T(256)}, u32[]{:S(2)}) copy-start(f32[256]{0:T(256)} %copy-done.25) | copy-start | bytes 3076
  (27 other events, 408.8 us)
Sparse Core Ops, SparseCore 0:
  10.5 30.9 all-gather.9
  60.4 123.8 all-gather.5
  186.2 45.1 all-gather.7
  233.7 54.3 all-gather.11
  290.4 55.9 all-gather.13
  385.3 41.9 reduce-scatter.16
  431.2 31.2 reduce-scatter.22
  465.9 62.1 reduce-scatter.14
  530.6 76.7 reduce-scatter.12
  609.5 78.3 reduce-scatter.10
  691.7 71.7 reduce-scatter.20
  766.9 71.2 reduce-scatter.18
